TPU v7x, 32 devices: a whole 2x2x4 slice. The times are simulated.
32 devices in a mesh: sec: 8 (over z, core), bond: 4 (over y, x).
Axes of the slice: x: 2, y: 2, z: 4, core: 2. Of those that a mesh axis runs over, the one named last changes fastest.
Arguments:
- left_env: bfloat16 [8, 512, 8, 512], P('sec', 'bond'), may hold values from -6 to 6
- site: bfloat16 [8, 512, 4, 512], P('sec', 'bond'), may hold values from -0.125 to 0.125
- psi: bfloat16 [8, 512, 4, 4, 512], P('sec', 'bond'), may hold values from -0.25 to 0.25
- right_env: bfloat16 [8, 8, 512, 512], P('sec'), may hold values from -0.09375 to 0.09375
- mpo: bfloat16 [8, 8, 4, 4], replicated, may hold values from -1 to 1
Outputs:
- new_left: bfloat16 [8, 512, 8, 512], P('sec', 'bond')
- product: bfloat16 [8, 512, 4, 4, 512], P('sec', 'bond')
All inputs are finite; a program needn't handle non-finite values.
Results may differ from a plain program's by a relative error of at most 0.0095.
Values may be sent and summed in bfloat16 or wider, within the bound.
A program may use at most 128 MiB of HBM per device.

v0:
```python
import jax
import jax.numpy as jnp
from jax import lax
from jax.sharding import PartitionSpec as P


def shifted(block, axis, distance):
    devices = range(lax.axis_size(axis))
    route = [((i - distance) % len(devices), i) for i in devices]
    return lax.ppermute(block, axis, route)


def shards(left_env, site, psi, right_env, mpo):
    left = left_env[0]
    tensor = site[0]
    rows = tensor.shape[0]
    phys = tensor.shape[1]
    chi = tensor.shape[2]
    width = left.shape[1]
    pair_source = shifted(psi[0], "sec", 1)
    offset = lax.axis_index("bond") * rows
    whole_left, whole_site = (
        lax.all_gather(left, "bond", axis=0, tiled=True),
        lax.all_gather(tensor, "bond", axis=0, tiled=True),
    )
    own_cols = lax.dynamic_slice_in_dim(whole_site, offset, rows, 2)
    first = jnp.dot(
        whole_left.reshape(chi * width, chi),
        own_cols.reshape(chi, phys * rows),
        preferred_element_type=jnp.float32,
    )
    first = first.astype(jnp.bfloat16).reshape(chi, width, phys, rows)
    second = jnp.einsum("pmsb,mnsu->punb", first, mpo, preferred_element_type=jnp.float32).astype(
        jnp.bfloat16
    )
    fresh = lax.dot_general(
        whole_site.reshape(chi * phys, chi),
        second.reshape(chi * phys, width * rows),
        (((0,), (0,)), ((), ())),
        preferred_element_type=jnp.float32,
    )
    fresh = fresh.astype(jnp.bfloat16).reshape(chi, width, rows)
    new_left = lax.all_to_all(fresh, "bond", split_axis=0, concat_axis=2, tiled=True)
    left_source = shifted(new_left, "sec", 1)
    source_flat = left_source.reshape(rows * width, chi)
    pair = pair_source.reshape(rows, phys * phys * chi)
    mixed = jnp.dot(
        source_flat,
        lax.all_gather(pair, "bond", axis=0, tiled=True),
        preferred_element_type=jnp.float32,
    )
    mixed = mixed.astype(jnp.bfloat16).reshape(rows, width * phys * phys, chi)
    two_site = jnp.einsum("mnsu,nkvw->msvuwk", mpo, mpo, preferred_element_type=jnp.float32)
    two_site = two_site.astype(jnp.bfloat16).reshape(width * phys * phys, phys * phys * width)
    projected = jnp.einsum(
        "pqc,qr->prc", mixed, two_site, preferred_element_type=jnp.float32
    ).astype(jnp.bfloat16)
    env_right = right_env[0].reshape(width * chi, chi)
    result = jnp.dot(
        projected.reshape(rows * phys * phys, width * chi),
        env_right,
        preferred_element_type=jnp.float32,
    ).astype(jnp.bfloat16)
    return (new_left[None], result.reshape(1, rows, phys, phys, chi))


def solution(mesh):
    in_specs = (
        P("sec", "bond", None, None),
        P("sec", "bond", None, None),
        P("sec", "bond", None, None, None),
        P("sec", None, None, None),
        P(),
    )
    out_specs = (P("sec", "bond", None, None), P("sec", "bond", None, None, None))
    return jax.shard_map(shards, mesh=mesh, in_specs=in_specs, out_specs=out_specs, check_vma=False)
```

profile of v0, /device:TPU:16, one launch (start us, length us, event | category | flops | bytes accessed | tf_op | source)
XLA Modules:
  0.0 301.9 jit_solution(9496560427606506454)
XLA Ops:
  7.2 0.0 copy-start.1
  7.2 0.0 all-gather.8.cloned.1.call-start
  7.2 0.7 all-gather.8.cloned.1.call-update
  7.9 0.0 all-gather.10.cloned.1.call-start
  8.0 0.7 all-gather.10.cloned.1.call-update
  8.7 0.0 all-gather.6.cloned.1.call-start
  8.7 0.1 collective-permute-start.1
  8.8 25.7 %collective-permute-done.1 = bf16[128,4,4,512]{3,2,1,0:T(4,128)(2,1)S(1)} collective-permute-done((bf16[128,4,4,512]{3,2,1,0:T(4,128)(2,1)}, bf16[128,4,4,512]{3,2,1,0:T(4,128)(2,1)S(1)}, u32[]{:S(2)}, u32[]{:S(2)}) %collective-permute-start.1) | collective-permute-done | bytes 2097184 | tf_op jit(solution)/shard_map/ppermute | solution.py:10
  34.4 2.8 reshape.49
  37.2 0.0 all-gather.6.cloned.1.call-update
  37.2 0.0 copy-done.1
  37.2 0.1 copy.51
  37.3 8.8 %all-gather.8.cloned.1.call-done = bf16[1,512,4,512]{3,2,0,1:T(4,128)(2,1)} async-done(((bf16[1,128,4,512]{3,2,0,1:T(4,128)(2,1)}), bf16[1,512,4,512]{3,2,0,1:T(4,128)(2,1)}) %all-gather.8.cloned.1.call-update) | async-done | bytes 2097168 | tf_op jit(solution)/shard_map/all_gather | solution.py:24
  46.1 2.5 reshape.45
  48.7 1.2 constant_dynamic-slice_fusion
  49.9 50.7 %all-gather.10.cloned.1.call-done = bf16[1,512,8,512]{3,2,0,1:T(8,128)(2,1)} async-done(((bf16[1,128,8,512]{3,2,0,1:T(8,128)(2,1)}), bf16[1,512,8,512]{3,2,0,1:T(8,128)(2,1)}) %all-gather.10.cloned.1.call-update) | async-done | bytes 4194320 | tf_op jit(solution)/shard_map/all_gather | solution.py:23
  100.6 6.6 %fusion = bf16[4096,512]{0,1:T(8,128)(2,1)} fusion(bf16[1,512,8,512]{3,2,0,1:T(8,128)(2,1)} %all-gather.10.cloned.1.call-done, bf16[64,8,4,128]{3,2,1,0:T(4,128)(2,1)S(1)} %bitcast.77), kind=kOutput, calls=%fused_computation.4 | convolution fusion | flops 2149580800 | bytes 8912896 | tf_op jit(solution)/shard_map/dot_general | solution.py:27
  107.1 6.6 %copy.50 = bf16[4096,512]{1,0:T(8,128)(2,1)} copy(bf16[4096,512]{0,1:T(8,128)(2,1)} %fusion) | data formatting | bytes 8388608 | tf_op jit(solution)/shard_map/convert_element_type | solution.py:32
  113.7 4.2 %bitcast_convert_fusion = bf16[512,128,8,4]{1,2,3,0:T(8,128)(2,1)S(1)} fusion(bf16[4096,512]{1,0:T(8,128)(2,1)} %copy.50, bf16[8,8,4,4]{0,1,2,3:T(8,128)(2,1)S(1)} %copy.51), kind=kOutput, calls=%fused_computation.2 | convolution fusion | flops 136314880 | bytes 8390656 | tf_op jit(solution)/shard_map/pmsb,mnsu->punb/dot_general | solution.py:33
  118.0 2.4 fusion.9
  120.3 0.8 copy.52
  121.1 27.9 %all_to_all.18 = bf16[512,8,128]{2,1,0:T(8,128)(2,1)S(1)} all-to-all(bf16[512,8,128]{2,1,0:T(8,128)(2,1)S(1)} %copy.52), channel_id=1, replica_groups=mesh['sec'=8,'bond'=4] {'bond'}, dimensions={0} | all-to-all | bytes 2097152 | tf_op jit(solution)/shard_map/all_to_all | solution.py:43
  149.0 0.2 copy.87
  149.1 0.0 copy-start
  149.2 0.2 collective-permute-start
  149.4 0.3 fusion.12
  149.8 0.9 copy.56
  150.7 0.5 reshape.47
  151.2 12.4 %collective-permute-done = bf16[128,8,512]{2,1,0:T(8,128)(2,1)S(1)} collective-permute-done((bf16[128,8,512]{2,1,0:T(8,128)(2,1)S(1)}, bf16[128,8,512]{2,1,0:T(8,128)(2,1)S(1)}, u32[]{:S(2)}, u32[]{:S(2)}) %collective-permute-start) | collective-permute-done | bytes 1048608 | tf_op jit(solution)/shard_map/ppermute | solution.py:10
  163.6 38.1 %all-gather.6.cloned.1.call-done = bf16[512,8192]{1,0:T(8,128)(2,1)} async-done(((bf16[128,8192]{1,0:T(8,128)(2,1)}), bf16[512,8192]{1,0:T(8,128)(2,1)}) %all-gather.6.cloned.1.call-update) | async-done | bytes 8388624 | tf_op jit(solution)/shard_map/all_gather | solution.py:49
  201.8 15.1 %convolution_convert_fusion = bf16[1024,8192]{1,0:T(8,128)(2,1)} fusion(bf16[512,8192]{1,0:T(8,128)(2,1)} %all-gather.6.cloned.1.call-done, bf16[128,8,512]{2,1,0:T(8,128)(2,1)S(1)} %collective-permute-done), kind=kOutput, calls=%fused_computation.1 | convolution fusion | flops 8598323200 | bytes 26214400 | tf_op jit(solution)/shard_map/dot_general | solution.py:47
  216.8 0.0 copy-done
  216.8 25.6 %reshape.50 = bf16[128,128,512]{2,1,0:T(8,128)(2,1)} reshape(bf16[1024,8192]{1,0:T(8,128)(2,1)} %convolution_convert_fusion) | data formatting | bytes 33554432 | tf_op jit(solution)/shard_map/reshape | solution.py:52
  242.5 11.7 %convert_bitcast_fusion = bf16[128,128,512]{2,1,0:T(8,128)(2,1)} fusion(bf16[128,128,512]{2,1,0:T(8,128)(2,1)} %reshape.50, bf16[128,128]{1,0:T(8,128)(2,1)S(1)} %reshape.47), kind=kOutput, calls=%fused_computation | convolution fusion | flops 2155872256 | bytes 33587200 | tf_op jit(solution)/shard_map/pqc,qr->prc/dot_general | solution.py:55
  254.1 25.6 %reshape.51 = bf16[2048,4096]{1,0:T(8,128)(2,1)} reshape(bf16[128,128,512]{2,1,0:T(8,128)(2,1)} %convert_bitcast_fusion) | data formatting | bytes 33554432 | tf_op jit(solution)/shard_map/reshape | solution.py:60
  279.8 13.6 %convolution_convert_fusion.2 = bf16[2048,512]{1,0:T(8,128)(2,1)S(1)} fusion(bf16[2048,4096]{1,0:T(8,128)(2,1)} %reshape.51, bf16[4096,512]{1,0:T(8,128)(2,1)} %bitcast.79), kind=kOutput, calls=%fused_computation.11 | convolution fusion | flops 8590983168 | bytes 23068672 | tf_op jit(solution)/shard_map/dot_general | solution.py:59
  293.3 2.0 reshape.52
Async XLA Ops:
  7.2 30.1 %copy-start.1 = (bf16[8,8,4,4]{1,3,2,0:T(4,128)(2,1)S(1)}, bf16[8,8,4,4]{1,3,2,0:T(4,128)(2,1)}, u32[]{:S(2)}) copy-start(bf16[8,8,4,4]{1,3,2,0:T(4,128)(2,1)} %param.9) | copy-start | bytes 6148
  7.2 38.9 %all-gather.8.cloned.1.call-start = ((), (), s32[]{:S(2)}) async-start(), calls=%async_computation.2 | async-start | bytes 2621440 | tf_op jit(solution)/shard_map/all_gather | solution.py:24
  7.9 92.6 %all-gather.10.cloned.1.call-start = ((), (), s32[]{:S(2)}) async-start(), calls=%async_computation.3 | async-start | bytes 5242880 | tf_op jit(solution)/shard_map/all_gather | solution.py:23
  8.7 193.1 %all-gather.6.cloned.1.call-start = ((), (), s32[]{:S(2)}) async-start(), calls=%async_computation.1 | async-start | bytes 10485760 | tf_op jit(solution)/shard_map/all_gather | solution.py:49
  8.7 25.7 %collective-permute-start.1 = (bf16[128,4,4,512]{3,2,1,0:T(4,128)(2,1)}, bf16[128,4,4,512]{3,2,1,0:T(4,128)(2,1)S(1)}, u32[]{:S(2)}, u32[]{:S(2)}) collective-permute-start(bf16[128,4,4,512]{3,2,1,0:T(4,128)(2,1)} %bitcast.80), channel_id=1, source_target_pairs={{28,0},{0,4},{4,8},{8,12},{12,16},{16,20},{20,24},{24,28},{29,1},{... | collective-permute-start | bytes 6291464 | tf_op jit(solution)/shard_map/ppermute | solution.py:10
  149.1 67.7 %copy-start = (bf16[128,8,4,128]{3,1,2,0:T(8,128)(2,1)}, bf16[128,8,4,128]{3,1,2,0:T(8,128)(2,1)S(1)}, u32[]{:S(2)}) copy-start(bf16[128,8,4,128]{3,1,2,0:T(8,128)(2,1)S(1)} %copy.87) | copy-start | bytes 3145732
  149.2 14.5 %collective-permute-start = (bf16[128,8,512]{2,1,0:T(8,128)(2,1)S(1)}, bf16[128,8,512]{2,1,0:T(8,128)(2,1)S(1)}, u32[]{:S(2)}, u32[]{:S(2)}) collective-permute-start(bf16[128,8,512]{2,1,0:T(8,128)(2,1)S(1)} %bitcast.73), channel_id=1, source_target_pairs={{28,0},{0,4},{4,8},{8,12},{12,16},{16,20},{20,24},{24,28},{29,1},{... | collective-permute-start | bytes 3145736 | tf_op jit(solution)/shard_map/ppermute | solution.py:10
Sparse Core Ops, SparseCore 0:
  9.8 36.2 all-gather.7
  47.9 52.5 all-gather.9
  103.0 98.7 all-gather.5
where the time goes:
time: 305 us; the launch traced here: 302 us
  waiting for transfers between devices  137 us (45%)
  local copies, waits for them, and re-layouts  68.9 us (23%)
  matrix products  53.8 us (18%)
  blocking collectives  27.9 us (9%)
  between operations  13.9 us (5%)
    all_gather x1, waiting for transfers between devices, shards(): lax.all_gather(left, 'bond', axis=0, tiled=True)  50.7 us
    all_gather x1, waiting for transfers between devices, shards(): lax.all_gather(pair, 'bond', axis=0, tiled=True)  38.1 us
    ppermute x2, waiting for transfers between devices, shifted(): return lax.ppermute(block, axis, route)  38.1 us
    all_to_all x1, blocking collectives, shards(): lax.all_to_all(fresh, 'bond', split_axis=0, concat_axis=2, tiled=True)  27.9 us
    reshape x1, local copies, waits for them, and re-layouts, shards(): mixed = mixed.astype(jnp.bfloat16).reshape(rows, width * phys * phys, chi)  25.6 us
    reshape x1, local copies, waits for them, and re-layouts, shards(): projected.reshape(rows * phys * phys, width * chi)  25.6 us
    dot_general x1, matrix products, shards(): jnp.dot(source_flat, lax.all_gather(pair, 'bond', axis=0, tiled=True), pr...  15.1 us
    dot_general x1, matrix products, shards(): jnp.dot(projected.reshape(rows * phys * phys, width * chi), env_right, pr...  13.6 us
  transfers between devices with their start and end apart: 5, of which 5 were waited for; matrix products, arithmetic and copies ran while one was open for 10% of the time, Pallas kernels for 0%

commit v1 on v0

--- a/solution.py
+++ b/solution.py
@@ -1,7 +1,296 @@
+import functools
+
 import jax
 import jax.numpy as jnp
 from jax import lax
+from jax.experimental import pallas as pl
+from jax.experimental.pallas import tpu as pltpu
 from jax.sharding import PartitionSpec as P
+
+MESH = pl.DeviceIdType.MESH
+BF16 = jnp.bfloat16
+F32 = jnp.float32
+
+
+def mm(a, b):
+    return jnp.dot(a, b, preferred_element_type=F32)
+
+
+def kernel(
+    dims,
+    left_h, site_h, site_tr_h, psi_h, right_h, mix_h, pair_h,
+    new_left, product,
+    left, site, site_tr, mix, pair, right,
+    second, part, rs1, send2, rs2, nl32, nl_in, psi, mixed, proj, acc,
+    local_sem, send_sem, recv_sem,
+):
+    rows, width, phys, chi, group, cuts, batch = dims
+    n_bond = 4
+    pq = phys * phys
+    step = chi // cuts
+    sec = lax.axis_index("sec")
+    me = lax.axis_index("bond")
+    n_sec = lax.axis_size("sec")
+    next_sec = lax.rem(sec + 1, n_sec)
+    prev_sec = lax.rem(sec + n_sec - 1, n_sec)
+    bx = (me // 2) * 2 + 1 - lax.rem(me, 2)
+    by = lax.rem(me + 2, n_bond)
+    bd = lax.rem(bx + 2, n_bond)
+    to_x = {"bond": bx}
+    to_y = {"bond": by}
+    to_next = {"sec": next_sec}
+
+    def block(owner):
+        return pl.ds(pl.multiple_of(owner * rows, rows), rows)
+
+    loads = {}
+    for i, (name, src, dst) in enumerate((
+        ("site", site_h, site.at[:, block(me), :]),
+        ("left", left_h, left),
+        ("mix", mix_h, mix),
+        ("site_tr", site_tr_h, site_tr),
+        ("pair", pair_h, pair),
+        ("right", right_h, right),
+    )):
+        loads[name] = pltpu.make_async_copy(src, dst, local_sem.at[i])
+        loads[name].start()
+
+    barrier = pltpu.get_barrier_semaphore()
+    for target in (to_x, to_y, to_next, {"sec": prev_sec}):
+        pl.semaphore_signal(barrier, inc=1, device_id=target, device_id_type=MESH)
+    pl.semaphore_wait(barrier, 4)
+
+    started = []
+    counter = {}
+
+    def slot(key):
+        return counter.setdefault(key, len(counter))
+
+    def send(key, src, dst, target):
+        i = slot(key)
+        copy = pltpu.make_async_remote_copy(
+            src_ref=src, dst_ref=dst, send_sem=send_sem.at[i], recv_sem=recv_sem.at[i],
+            device_id=target, device_id_type=MESH,
+        )
+        copy.start()
+        started.append(copy)
+
+    def arrive(key, dst, target):
+        i = slot(key)
+        pltpu.make_async_remote_copy(
+            src_ref=dst, dst_ref=dst, send_sem=send_sem.at[i], recv_sem=recv_sem.at[i],
+            device_id=target, device_id_type=MESH,
+        ).wait_recv()
+
+    half_s = phys // 2
+    send("site_x", site_h, site.at[:, block(me), :], to_x)
+    send("site_y", site_h, site.at[:, block(me), :], to_y)
+
+    chunks = [(cc, h) for cc in range(cuts) for h in range(2)]
+    hp = pq // 2
+    qp = hp // 2
+
+    def region(q, owner, sub=None):
+        cc, h = chunks[q]
+        if sub is None:
+            return psi.at[cc, pl.ds(h * hp, hp), block(owner), :]
+        return psi.at[cc, pl.ds(h * hp + sub * qp, qp), block(owner), :]
+
+    for q, (cc, h) in enumerate(chunks):
+        send(("shift", q), psi_h.at[cc, pl.ds(h * hp, hp)], region(q, me), to_next)
+
+    def spread(q):
+        arrive(("shift", q), region(q, me), to_next)
+        send(("psi_x", q), region(q, me), region(q, me), to_x)
+        send(("psi_y", q), region(q, me), region(q, me), to_y)
+
+    def relay(q):
+        arrive(("psi_x", q), region(q, bx), to_x)
+        send(("psi_xy", q), region(q, bx, 0), region(q, bx, 0), to_y)
+        arrive(("psi_y", q), region(q, by), to_y)
+        send(("psi_yx", q), region(q, by, 1), region(q, by, 1), to_x)
+
+    def complete(q):
+        arrive(("psi_xy", q), region(q, bd, 0), to_y)
+        arrive(("psi_yx", q), region(q, bd, 1), to_x)
+
+    lo, hi = pl.ds(0, half_s), pl.ds(half_s, phys - half_s)
+    arrive("site_x", site.at[:, block(bx), :], to_x)
+    send("site_xy", site.at[lo, block(bx), :], site.at[lo, block(bx), :], to_y)
+    arrive("site_y", site.at[:, block(by), :], to_y)
+    send("site_yx", site.at[hi, block(by), :], site.at[hi, block(by), :], to_x)
+    spread(0)
+    loads["site"].wait()
+    loads["left"].wait()
+    loads["mix"].wait()
+    loads["site_tr"].wait()
+    arrive("site_xy", site.at[lo, block(bd), :], to_y)
+    arrive("site_yx", site.at[hi, block(bd), :], to_x)
+
+    strip = group * width
+
+    @pl.loop(0, rows // group)
+    def _(g):
+        ours = left[pl.ds(pl.multiple_of(g * strip, strip), strip), :]
+        first = jnp.concatenate([mm(ours, site[s]).astype(BF16) for s in range(phys)], axis=0)
+        out = mm(mix[...], first).astype(BF16)
+        for u in range(phys):
+            for n in range(width):
+                at = (u * width + n) * group
+                where = pl.multiple_of(u * rows + g * group, group)
+                second[n, pl.ds(where, group), :] = out[at:at + group, :]
+
+    relay(0)
+    half_w = width // 2
+    order = [k + d * half_w for k in range(half_w) for d in range(2)]
+
+    def first_round(n):
+        if n < half_w:
+            send(("rs_own", n), part.at[n, block(bx), :], rs1.at[n, 0], to_x)
+            send(("rs_far", n), part.at[n, block(bd), :], rs1.at[n, 1], to_x)
+        else:
+            send(("rs_own", n), part.at[n, block(by), :], rs1.at[n, 0], to_y)
+            send(("rs_far", n), part.at[n, block(bd), :], rs1.at[n, 1], to_y)
+
+    behind = None
+    for n in order:
+        part[n] = mm(site_tr[...], second[n]).astype(BF16)
+        if behind is not None:
+            first_round(behind)
+        behind = n
+    first_round(behind)
+    spread(1)
+
+    def second_round(n):
+        if n < half_w:
+            send(("rs_last", n), send2.at[n], rs2.at[n], to_y)
+        else:
+            send(("rs_last", n), send2.at[n], rs2.at[n], to_x)
+
+    behind = None
+    for n in order:
+        src, other = (to_x, by) if n < half_w else (to_y, bx)
+        arrive(("rs_far", n), rs1.at[n, 1], src)
+        send2[n] = (part[n, block(other), :].astype(F32) + rs1[n, 1].astype(F32)).astype(BF16)
+        if behind is not None:
+            second_round(behind)
+        behind = n
+    second_round(behind)
+    relay(1)
+    spread(2)
+    for n in order:
+        src, last = (to_x, to_y) if n < half_w else (to_y, to_x)
+        arrive(("rs_own", n), rs1.at[n, 0], src)
+        arrive(("rs_last", n), rs2.at[n], last)
+        total = part[n, block(me), :].astype(F32) + rs1[n, 0].astype(F32) + rs2[n].astype(F32)
+        for i in range(chi // 128):
+            nl32[i, pl.ds(n, rows, stride=width), :] = total[:, i * 128:(i + 1) * 128]
+    for i in range(chi // 128):
+        new_left[:, i * 128:(i + 1) * 128] = nl32[i].astype(BF16)
+    send("left", new_left, nl_in, to_next)
+    relay(2)
+    spread(3)
+    complete(0)
+    complete(1)
+    loads["pair"].wait()
+    loads["right"].wait()
+    arrive("left", nl_in, to_next)
+
+    for cc in range(cuts):
+        if cc == 1:
+            complete(2)
+            complete(3)
+
+        @pl.loop(0, rows // batch)
+        def _(g):
+            tall = batch * width
+            ours = nl_in[pl.ds(pl.multiple_of(g * tall, tall), tall), :]
+
+            @pl.loop(0, pq)
+            def _(s):
+                mixed[s] = mm(ours, psi[cc, s])
+
+            @pl.loop(0, batch, unroll=4)
+            def _(p):
+                here = mixed[:, pl.ds(pl.multiple_of(p * width, width), width), :]
+                out = mm(pair[...], here.reshape(pq * width, step).astype(BF16)).astype(BF16)
+                for k in range(width):
+                    proj[k, pl.ds(pl.multiple_of(p * pq, pq), pq), :] = out[k * pq:(k + 1) * pq, :]
+
+            total = mm(proj[0], right[0, pl.ds(cc * step, step), :])
+            for k in range(1, width):
+                total += mm(proj[k], right[k, pl.ds(cc * step, step), :])
+            long = pl.ds(pl.multiple_of(g * batch * pq, batch * pq), batch * pq)
+            if cc > 0:
+                total += acc[long, :]
+            if cc < cuts - 1:
+                acc[long, :] = total
+            else:
+                product[long, :] = total.astype(BF16)
+
+        if cc == 0:
+            relay(3)
+
+    for copy in started:
+        copy.wait_send()
+
+
+def fused(left_env, site, psi, right_env, mpo):
+    _, rows, width, chi = left_env.shape
+    phys = site.shape[2]
+    pq = phys * phys
+    group, cuts, batch = 16, 2, 32
+    step = chi // cuts
+    by_phys = site[0].transpose(1, 0, 2)
+    site_tr = by_phys.reshape(phys * rows, chi).T
+    pairs = psi[0].reshape(rows, pq, cuts, step).transpose(2, 1, 0, 3)
+    eye = jnp.eye(group, dtype=BF16)
+    mix = (
+        mpo.transpose(3, 1, 2, 0)[:, :, None, :, None, :] * eye[None, None, :, None, :, None]
+    ).reshape(phys * width * group, phys * group * width)
+    pair = jnp.einsum("mnsu,nkvw->kuwsvm", mpo, mpo, preferred_element_type=F32)
+    pair = pair.astype(BF16).reshape(width * pq, pq * width)
+    n_sems = 80
+    any_spec = pl.BlockSpec(memory_space=pl.ANY)
+    vmem = pl.BlockSpec(memory_space=pltpu.VMEM)
+    new_left, product = pl.pallas_call(
+        functools.partial(kernel, (rows, width, phys, chi, group, cuts, batch)),
+        out_shape=(
+            jax.ShapeDtypeStruct((rows * width, chi), BF16),
+            jax.ShapeDtypeStruct((rows * pq, chi), BF16),
+        ),
+        in_specs=[any_spec] * 7,
+        out_specs=(vmem, vmem),
+        scratch_shapes=[
+            pltpu.VMEM((rows * width, chi), BF16),
+            pltpu.VMEM((phys, chi, chi), BF16),
+            pltpu.VMEM((chi, phys * rows), BF16),
+            pltpu.VMEM(mix.shape, BF16),
+            pltpu.VMEM(pair.shape, BF16),
+            pltpu.VMEM((width, chi, chi), BF16),
+            pltpu.VMEM((width, phys * rows, chi), BF16),
+            pltpu.VMEM((width, chi, chi), BF16),
+            pltpu.VMEM((width, 2, rows, chi), BF16),
+            pltpu.VMEM((width, rows, chi), BF16),
+            pltpu.VMEM((width, rows, chi), BF16),
+            pltpu.VMEM((chi // 128, rows * width, 128), F32),
+            pltpu.VMEM((rows * width, chi), BF16),
+            pltpu.VMEM((cuts, pq, chi, step), BF16),
+            pltpu.VMEM((pq, batch * width, step), F32),
+            pltpu.VMEM((width, batch * pq, step), BF16),
+            pltpu.VMEM((rows * pq, chi), F32),
+            pltpu.SemaphoreType.DMA((6,)),
+            pltpu.SemaphoreType.DMA((n_sems,)),
+            pltpu.SemaphoreType.DMA((n_sems,)),
+        ],
+        compiler_params=pltpu.CompilerParams(
+            collective_id=0, has_side_effects=True, vmem_limit_bytes=62 * 1024 * 1024
+        ),
+    )(left_env[0].reshape(rows * width, chi), by_phys, site_tr, pairs, right_env[0], mix, pair)
+    return (
+        new_left.reshape(1, rows, width, chi),
+        product.reshape(1, rows, phys, phys, chi),
+    )
 
 
 def shifted(block, axis, distance):
@@ -73,4 +362,5 @@
         P(),
     )
     out_specs = (P("sec", "bond", None, None), P("sec", "bond", None, None, None))
-    return jax.shard_map(shards, mesh=mesh, in_specs=in_specs, out_specs=out_specs, check_vma=False)
+    body = fused if mesh.shape["bond"] == 4 else shards
+    return jax.shard_map(body, mesh=mesh, in_specs=in_specs, out_specs=out_specs, check_vma=False)

time: 305 us -> 197 us (0.65)
  Pallas kernels: 0 us -> 168 us
  waiting for transfers between devices: 137 us -> 0 us
  matrix products: 53.8 us -> 0.35 us
  local copies, waits for them, and re-layouts: 68.9 us -> 23.5 us
  blocking collectives: 27.9 us -> 0 us
  between operations: 13.9 us -> 0.7 us
  other arithmetic: 0 us -> 3.93 us
    pallas_call x0 -> x1, Pallas kernels: none -> 168 us  [fused(): pl.pallas_call(functools.partial(kernel, (rows, width, phys, chi, group,...]
    all_gather x3 -> x0, waiting for transfers between devices: 97.6 us -> none  [the longest x1 50.7 us: shards(): lax.all_gather(left, 'bond', axis=0, tiled=True)]
    reshape x7 -> x3, local copies, waits for them, and re-layouts: 59.8 us -> 6.17 us  [the longest x1 4.05 us: fused(): product.reshape(1, rows, phys, phys, chi)]
    dot_general x7 -> x1, matrix products: 53.8 us -> 0.35 us  [fused(): pair = jnp.einsum('mnsu,nkvw->kuwsvm', mpo, mpo, preferred_element_type=F32)]
    ppermute x2 -> x0, waiting for transfers between devices: 38.1 us -> none  [shifted(): return lax.ppermute(block, axis, route)]
    all_to_all x1 -> x0, blocking collectives: 27.9 us -> none  [shards(): lax.all_to_all(fresh, 'bond', split_axis=0, concat_axis=2, tiled=True)]
    mul x0 -> x2, local copies, waits for them, and re-layouts: none -> 8.77 us  [fused(): mpo.transpose(3, 1, 2, 0)[:, :, None, :, None, :]]
    convert_element_type x2 -> x1, local copies, waits for them, and re-layouts: 7.56 us -> 0.41 us  [fused(): pair = pair.astype(BF16).reshape(width * pq, pq * width)]
  transfers between devices with their start and end apart: 5 -> 0, of which waited for: 5 -> 0; matrix products, arithmetic and copies ran while one was open for 10% -> 0% of each run, Pallas kernels for 0% -> 0%
where the time goes in v1:
time: 197 us; the launch traced here: 196 us
  Pallas kernels  168 us (85%)
  local copies, waits for them, and re-layouts  23.5 us (12%)
  other arithmetic  3.93 us (2%)
    pallas_call x1, Pallas kernels, fused(): pl.pallas_call(functools.partial(kernel, (rows, width, phys, chi, group,...  168 us
    mul x2, local copies, waits for them, and re-layouts, fused(): mpo.transpose(3, 1, 2, 0)[:, :, None, :, None, :]  8.77 us
    unnamed x9, local copies, waits for them, and re-layouts  5.55 us
    reshape x1, local copies, waits for them, and re-layouts, fused(): product.reshape(1, rows, phys, phys, chi)  4.05 us

profile of v1, /device:TPU:16, one launch (start us, length us, event | category | flops | bytes accessed | tf_op | source)
XLA Modules:
  0.0 196.4 jit_solution(13245852492891078537)
XLA Ops:
  0.6 1.1 copy.37
  1.8 0.0 copy-start
  1.8 1.0 copy.24
  2.8 3.9 %broadcast_multiply_fusion = bf16[4,8,16,4,16,8]{2,1,0,5,4,3:T(8,128)(2,1)} fusion(bf16[16,16]{0,1:T(8,128)(2,1)S(1)} %fusion.3, bf16[8,8,4,4]{1,3,2,0:T(4,128)(2,1)} %param.9), kind=kLoop, calls=%fused_computation | loop fusion | flops 1048576 | bytes 526848 | tf_op jit(solution)/shard_map/mul | solution.py:249
  6.7 7.8 %mul.20 = bf16[512,512]{0,1:T(8,128)(2,1)S(1)} reshape(bf16[4,8,16,4,16,8]{2,1,0,5,4,3:T(8,128)(2,1)} %broadcast_multiply_fusion) | data formatting | bytes 1048576 | tf_op jit(solution)/shard_map/mul | solution.py:249
  14.5 0.0 copy-done
  14.5 1.0 copy.21.mix_h
  15.5 0.0 copy-start.2
  15.5 3.4 %copy.15 = bf16[1,128,4,4,512]{1,4,3,2,0:T(8,128)(2,1)S(1)} copy(bf16[1,128,4,4,512]{4,3,2,1,0:T(4,128)(2,1)} %param.7) | data formatting | bytes 4194304 | tf_op args[2]
  19.0 2.6 %copy.16 = bf16[128,16,2,256]{3,0,1,2:T(8,128)(2,1)} copy(bf16[128,16,2,256]{0,3,2,1:T(8,128)(2,1)S(1)} %bitcast.28) | data formatting | bytes 4194304 | tf_op jit(solution)/shard_map/reshape;squeeze | solution.py:246
  21.6 0.0 copy-done.2
  21.6 0.3 fusion
  21.9 0.4 copy.20
  22.3 1.1 reshape.30.pair_h
  23.4 168.0 %shard_map.68 = (bf16[1024,512]{1,0:T(8,128)(2,1)}, bf16[2048,512]{1,0:T(8,128)(2,1)}) custom-call(bf16[1024,512]{1,0:T(8,128)(2,1)} %bitcast.33, bf16[4,128,512]{2,1,0:T(8,128)(2,1)} %bitcast.30, bf16[512,512]{1,0:T(8,128)(2,1)} %bitcast.32, bf16[2,16,128,256]{3,2,1,0:T(8,128)(2,1)} %bitcast.27, bf16[8,512,512]{2,1,0:T(8,128)(2,1)} %bitcast.31, ...), custom_call_target="tpu_custom_call" | custom-call | tf_op jit(solution)/shard_map/pallas_call | solution.py:256
  191.4 0.0 copy-start.1
  191.4 4.0 %reshape.32 = bf16[1,128,4,4,512]{4,3,2,1,0:T(4,128)(2,1)} reshape(bf16[2048,512]{1,0:T(8,128)(2,1)} %get-tuple-element.5) | data formatting | bytes 4194304 | tf_op jit(solution)/shard_map/reshape | solution.py:292
  195.5 0.0 copy-done.1
  195.5 1.0 copy.39
  (1 shorter events, 0.0 us)
Async XLA Ops:
  1.8 12.7 %copy-start = (bf16[1,128,4,512]{3,1,2,0:T(8,128)(2,1)}, bf16[1,128,4,512]{3,1,2,0:T(8,128)(2,1)S(1)}, u32[]{:S(2)}) copy-start(bf16[1,128,4,512]{3,1,2,0:T(8,128)(2,1)S(1)} %copy.37) | copy-start | bytes 1572868
  15.5 6.0 %copy-start.2 = (bf16[8,8,4,4]{1,3,2,0:T(4,128)(2,1)S(1)}, bf16[8,8,4,4]{1,3,2,0:T(4,128)(2,1)}, u32[]{:S(2)}) copy-start(bf16[8,8,4,4]{1,3,2,0:T(4,128)(2,1)} %param.9) | copy-start | bytes 6148
  191.4 4.1 %copy-start.1 = (bf16[1024,512]{1,0:T(8,128)(2,1)S(1)}, bf16[1024,512]{1,0:T(8,128)(2,1)}, u32[]{:S(2)}) copy-start(bf16[1024,512]{1,0:T(8,128)(2,1)} %get-tuple-element.4) | copy-start | bytes 3145732

commit v2 on v1

--- a/solution.py
+++ b/solution.py
@@ -18,16 +18,16 @@
 
 def kernel(
     dims,
-    left_h, site_h, site_tr_h, psi_h, right_h, mix_h, pair_h,
+    left_h, site_h, psi_h, right_h, mpo_h,
     new_left, product,
-    left, site, site_tr, mix, pair, right,
-    second, part, rs1, send2, rs2, nl32, nl_in, psi, mixed, proj, acc,
+    left, site_raw, psi_raw, mpo, right,
+    site_own, psi_own, site, site_tr, mix, pair,
+    second, part, rs1, send2, rs2, nl_own, nl_in, psi, mixed, proj, acc,
     local_sem, send_sem, recv_sem,
 ):
     rows, width, phys, chi, group, cuts, batch = dims
     n_bond = 4
     pq = phys * phys
-    step = chi // cuts
     sec = lax.axis_index("sec")
     me = lax.axis_index("bond")
     n_sec = lax.axis_size("sec")
@@ -45,11 +45,10 @@
 
     loads = {}
     for i, (name, src, dst) in enumerate((
-        ("site", site_h, site.at[:, block(me), :]),
+        ("site", site_h, site_raw),
+        ("psi", psi_h, psi_raw),
+        ("mpo", mpo_h, mpo),
         ("left", left_h, left),
-        ("mix", mix_h, mix),
-        ("site_tr", site_tr_h, site_tr),
-        ("pair", pair_h, pair),
         ("right", right_h, right),
     )):
         loads[name] = pltpu.make_async_copy(src, dst, local_sem.at[i])
@@ -82,22 +81,48 @@
             device_id=target, device_id_type=MESH,
         ).wait_recv()
 
-    half_s = phys // 2
-    send("site_x", site_h, site.at[:, block(me), :], to_x)
-    send("site_y", site_h, site.at[:, block(me), :], to_y)
-
-    chunks = [(cc, h) for cc in range(cuts) for h in range(2)]
-    hp = pq // 2
-    qp = hp // 2
+    lanes = chi // cuts
+
+    loads["site"].wait()
+    flat = site_raw[...].astype(F32).reshape(rows * phys, chi)
+    for i in range(cuts):
+        acc[i, :rows * phys, :] = flat[:, i * lanes:(i + 1) * lanes]
+    for t in range(phys):
+        for i in range(cuts):
+            tile = acc[i, pl.ds(t, rows, stride=phys), :]
+            site_own[t, :, i * lanes:(i + 1) * lanes] = tile.astype(BF16)
+            site_tr[i * lanes:(i + 1) * lanes, t * rows:(t + 1) * rows] = tile.T.astype(BF16)
+    site_here = pltpu.make_async_copy(site_own, site.at[:, block(me), :], local_sem.at[5])
+    site_here.start()
+    send("site_x", site_own, site.at[:, block(me), :], to_x)
+    send("site_y", site_own, site.at[:, block(me), :], to_y)
+
+    loads["psi"].wait()
+    tall = 8
+
+    @pl.loop(0, rows // tall)
+    def _(g):
+        flat = psi_raw[pl.ds(pl.multiple_of(g * tall, tall), tall)].astype(F32)
+        flat = flat.reshape(tall * pq, chi)
+        where = pl.ds(pl.multiple_of(g * tall * pq, tall * pq), tall * pq)
+        for i in range(cuts):
+            acc[i, where, :] = flat[:, i * lanes:(i + 1) * lanes]
+
+    half = pq // 4
 
     def region(q, owner, sub=None):
-        cc, h = chunks[q]
         if sub is None:
-            return psi.at[cc, pl.ds(h * hp, hp), block(owner), :]
-        return psi.at[cc, pl.ds(h * hp + sub * qp, qp), block(owner), :]
-
-    for q, (cc, h) in enumerate(chunks):
-        send(("shift", q), psi_h.at[cc, pl.ds(h * hp, hp)], region(q, me), to_next)
+            return psi.at[q, :, block(owner), :]
+        return psi.at[q, pl.ds(sub * half, half), block(owner), :]
+
+    for q in range(cuts):
+        for t in range(pq):
+            at = (t % 2) * lanes
+            tile = acc[q, pl.ds(t, rows, stride=pq), :]
+            psi_own[q, t // 2, :, at:at + lanes] = tile.astype(BF16)
+        if q > 0:
+            send(("shift", q - 1), psi_own.at[q - 1], region(q - 1, me), to_next)
+    send(("shift", cuts - 1), psi_own.at[cuts - 1], region(cuts - 1, me), to_next)
 
     def spread(q):
         arrive(("shift", q), region(q, me), to_next)
@@ -114,16 +139,50 @@
         arrive(("psi_xy", q), region(q, bd, 0), to_y)
         arrive(("psi_yx", q), region(q, bd, 1), to_x)
 
-    lo, hi = pl.ds(0, half_s), pl.ds(half_s, phys - half_s)
+    loads["mpo"].wait()
+
+    def iota(shape, axis):
+        return lax.broadcasted_iota(jnp.int32, shape, axis)
+
+    def one_hot(condition):
+        return jnp.where(condition, 1.0, 0.0).astype(BF16)
+
+    small = phys * width
+    big = small * group
+    tall_code = lax.div(iota((big, small), 0), group)
+    spread_rows = one_hot(tall_code == iota((big, small), 1))
+    col = iota((small, big), 1)
+    col_code = lax.div(col, group * width) * width + lax.rem(col, width)
+    spread_cols = one_hot(col_code == iota((small, big), 0))
+    wide = mm(mm(spread_rows, mpo[...]).astype(BF16), spread_cols)
+    same = lax.rem(iota((big, big), 0), group) == lax.rem(lax.div(iota((big, big), 1), width), group)
+    mix[...] = jnp.where(same, wide, 0.0).astype(BF16)
+
+    side = width * pq
+    col = iota((small, side), 1)
+    col_m = lax.rem(col, width)
+    col_sv = lax.rem(lax.div(col, width), pq // 2) * 2 + lax.div(col, width * (pq // 2))
+    col_s, col_v = lax.div(col_sv, phys), lax.rem(col_sv, phys)
+    row = iota((side, small), 0)
+    row_k, row_u, row_w = lax.div(row, pq), lax.rem(lax.div(row, phys), phys), lax.rem(row, phys)
+    code_c, code_r = iota((small, side), 0), iota((side, small), 1)
+    t1 = mm(mpo[...], one_hot(col_s * width + col_m == code_c)).astype(BF16)
+    t2 = mm(one_hot(row_w * width + row_k == code_r), mpo[...]).astype(BF16)
+    both = jnp.zeros((side, side), F32)
+    for n in range(width):
+        near = mm(one_hot(row_u * width + n == code_r), t1)
+        both += near * mm(t2, one_hot(col_v * width + n == code_c))
+    pair[...] = both.astype(BF16)
+
+    cut_s = phys // 2
+    lo, hi = pl.ds(0, cut_s), pl.ds(cut_s, phys - cut_s)
     arrive("site_x", site.at[:, block(bx), :], to_x)
     send("site_xy", site.at[lo, block(bx), :], site.at[lo, block(bx), :], to_y)
     arrive("site_y", site.at[:, block(by), :], to_y)
     send("site_yx", site.at[hi, block(by), :], site.at[hi, block(by), :], to_x)
     spread(0)
-    loads["site"].wait()
     loads["left"].wait()
-    loads["mix"].wait()
-    loads["site_tr"].wait()
+    site_here.wait()
     arrive("site_xy", site.at[lo, block(bd), :], to_y)
     arrive("site_yx", site.at[hi, block(bd), :], to_x)
 
@@ -131,7 +190,8 @@
 
     @pl.loop(0, rows // group)
     def _(g):
-        ours = left[pl.ds(pl.multiple_of(g * strip, strip), strip), :]
+        ours = left[pl.ds(pl.multiple_of(g * group, group), group)].astype(F32)
+        ours = ours.reshape(strip, chi).astype(BF16)
         first = jnp.concatenate([mm(ours, site[s]).astype(BF16) for s in range(phys)], axis=0)
         out = mm(mix[...], first).astype(BF16)
         for u in range(phys):
@@ -183,52 +243,57 @@
         arrive(("rs_own", n), rs1.at[n, 0], src)
         arrive(("rs_last", n), rs2.at[n], last)
         total = part[n, block(me), :].astype(F32) + rs1[n, 0].astype(F32) + rs2[n].astype(F32)
-        for i in range(chi // 128):
-            nl32[i, pl.ds(n, rows, stride=width), :] = total[:, i * 128:(i + 1) * 128]
-    for i in range(chi // 128):
-        new_left[:, i * 128:(i + 1) * 128] = nl32[i].astype(BF16)
-    send("left", new_left, nl_in, to_next)
+        for i in range(cuts):
+            acc[i, pl.ds(n, rows, stride=width), :] = total[:, i * lanes:(i + 1) * lanes]
+    whole = jnp.concatenate([acc[i, :rows * width, :] for i in range(cuts)], axis=1)
+    nl_own[...] = whole.astype(BF16)
+    new_left[...] = whole.reshape(rows, width, chi).astype(BF16)
+    send("left", nl_own, nl_in, to_next)
     relay(2)
     spread(3)
-    complete(0)
-    complete(1)
-    loads["pair"].wait()
     loads["right"].wait()
     arrive("left", nl_in, to_next)
 
-    for cc in range(cuts):
-        if cc == 1:
-            complete(2)
-            complete(3)
+    for q in range(cuts):
+        complete(q)
 
         @pl.loop(0, rows // batch)
         def _(g):
-            tall = batch * width
-            ours = nl_in[pl.ds(pl.multiple_of(g * tall, tall), tall), :]
-
-            @pl.loop(0, pq)
-            def _(s):
-                mixed[s] = mm(ours, psi[cc, s])
-
-            @pl.loop(0, batch, unroll=4)
+            high = batch * width
+            ours = nl_in[pl.ds(pl.multiple_of(g * high, high), high), :]
+
+            @pl.loop(0, pq // 2)
+            def _(t):
+                mixed[t] = mm(ours, psi[q, t])
+
+            @pl.loop(0, batch // 2, unroll=4)
             def _(p):
-                here = mixed[:, pl.ds(pl.multiple_of(p * width, width), width), :]
-                out = mm(pair[...], here.reshape(pq * width, step).astype(BF16)).astype(BF16)
-                for k in range(width):
-                    proj[k, pl.ds(pl.multiple_of(p * pq, pq), pq), :] = out[k * pq:(k + 1) * pq, :]
-
-            total = mm(proj[0], right[0, pl.ds(cc * step, step), :])
-            for k in range(1, width):
-                total += mm(proj[k], right[k, pl.ds(cc * step, step), :])
+                here = mixed[:, pl.ds(pl.multiple_of(p * 2 * width, 2 * width), 2 * width), :]
+                tiles = []
+                for i in range(2):
+                    one = here[:, i * width:(i + 1) * width, :].reshape(pq // 2 * width, 2 * lanes)
+                    tiles.append(jnp.concatenate([one[:, :lanes], one[:, lanes:]], axis=0))
+                both = jnp.concatenate(tiles, axis=1).astype(BF16)
+                out = mm(pair[...], both).astype(BF16)
+                for i in range(2):
+                    where = pl.ds(pl.multiple_of((p * 2 + i) * pq, pq), pq)
+                    for k in range(width):
+                        piece = out[k * pq:(k + 1) * pq, i * lanes:(i + 1) * lanes]
+                        proj[where, k * lanes:(k + 1) * lanes] = piece
+
+            env = right[:, q * lanes:(q + 1) * lanes, :].reshape(width * lanes, chi)
+            total = mm(proj[...], env)
             long = pl.ds(pl.multiple_of(g * batch * pq, batch * pq), batch * pq)
-            if cc > 0:
-                total += acc[long, :]
-            if cc < cuts - 1:
-                acc[long, :] = total
+            if q > 0:
+                total += jnp.concatenate([acc[i, long, :] for i in range(cuts)], axis=1)
+            if q < cuts - 1:
+                for i in range(cuts):
+                    acc[i, long, :] = total[:, i * lanes:(i + 1) * lanes]
             else:
-                product[long, :] = total.astype(BF16)
-
-        if cc == 0:
+                out = total.reshape(batch, phys, phys, chi).astype(BF16)
+                product[pl.ds(pl.multiple_of(g * batch, batch), batch)] = out
+
+        if q == 1:
             relay(3)
 
     for copy in started:
@@ -239,46 +304,44 @@
     _, rows, width, chi = left_env.shape
     phys = site.shape[2]
     pq = phys * phys
-    group, cuts, batch = 16, 2, 32
-    step = chi // cuts
-    by_phys = site[0].transpose(1, 0, 2)
-    site_tr = by_phys.reshape(phys * rows, chi).T
-    pairs = psi[0].reshape(rows, pq, cuts, step).transpose(2, 1, 0, 3)
-    eye = jnp.eye(group, dtype=BF16)
-    mix = (
-        mpo.transpose(3, 1, 2, 0)[:, :, None, :, None, :] * eye[None, None, :, None, :, None]
-    ).reshape(phys * width * group, phys * group * width)
-    pair = jnp.einsum("mnsu,nkvw->kuwsvm", mpo, mpo, preferred_element_type=F32)
-    pair = pair.astype(BF16).reshape(width * pq, pq * width)
+    group, cuts, batch = 16, 4, 64
+    lanes = chi // cuts
+    small = phys * width
+    table = mpo.transpose(3, 1, 2, 0).reshape(small, small)
     n_sems = 80
     any_spec = pl.BlockSpec(memory_space=pl.ANY)
     vmem = pl.BlockSpec(memory_space=pltpu.VMEM)
     new_left, product = pl.pallas_call(
         functools.partial(kernel, (rows, width, phys, chi, group, cuts, batch)),
         out_shape=(
-            jax.ShapeDtypeStruct((rows * width, chi), BF16),
-            jax.ShapeDtypeStruct((rows * pq, chi), BF16),
+            jax.ShapeDtypeStruct((rows, width, chi), BF16),
+            jax.ShapeDtypeStruct((rows, phys, phys, chi), BF16),
         ),
-        in_specs=[any_spec] * 7,
+        in_specs=[any_spec] * 5,
         out_specs=(vmem, vmem),
         scratch_shapes=[
-            pltpu.VMEM((rows * width, chi), BF16),
+            pltpu.VMEM((rows, width, chi), BF16),
+            pltpu.VMEM((rows, phys, chi), BF16),
+            pltpu.VMEM((rows, phys, phys, chi), BF16),
+            pltpu.VMEM((small, small), BF16),
+            pltpu.VMEM((width, chi, chi), BF16),
+            pltpu.VMEM((phys, rows, chi), BF16),
+            pltpu.VMEM((cuts, pq // 2, rows, 2 * lanes), BF16),
             pltpu.VMEM((phys, chi, chi), BF16),
             pltpu.VMEM((chi, phys * rows), BF16),
-            pltpu.VMEM(mix.shape, BF16),
-            pltpu.VMEM(pair.shape, BF16),
-            pltpu.VMEM((width, chi, chi), BF16),
+            pltpu.VMEM((small * group, small * group), BF16),
+            pltpu.VMEM((width * pq, width * pq), BF16),
             pltpu.VMEM((width, phys * rows, chi), BF16),
             pltpu.VMEM((width, chi, chi), BF16),
             pltpu.VMEM((width, 2, rows, chi), BF16),
             pltpu.VMEM((width, rows, chi), BF16),
             pltpu.VMEM((width, rows, chi), BF16),
-            pltpu.VMEM((chi // 128, rows * width, 128), F32),
             pltpu.VMEM((rows * width, chi), BF16),
-            pltpu.VMEM((cuts, pq, chi, step), BF16),
-            pltpu.VMEM((pq, batch * width, step), F32),
-            pltpu.VMEM((width, batch * pq, step), BF16),
-            pltpu.VMEM((rows * pq, chi), F32),
+            pltpu.VMEM((rows * width, chi), BF16),
+            pltpu.VMEM((cuts, pq // 2, chi, 2 * lanes), BF16),
+            pltpu.VMEM((pq // 2, batch * width, 2 * lanes), F32),
+            pltpu.VMEM((batch * pq, width * lanes), BF16),
+            pltpu.VMEM((cuts, rows * pq, lanes), F32),
             pltpu.SemaphoreType.DMA((6,)),
             pltpu.SemaphoreType.DMA((n_sems,)),
             pltpu.SemaphoreType.DMA((n_sems,)),
@@ -286,11 +349,8 @@
         compiler_params=pltpu.CompilerParams(
             collective_id=0, has_side_effects=True, vmem_limit_bytes=62 * 1024 * 1024
         ),
-    )(left_env[0].reshape(rows * width, chi), by_phys, site_tr, pairs, right_env[0], mix, pair)
-    return (
-        new_left.reshape(1, rows, width, chi),
-        product.reshape(1, rows, phys, phys, chi),
-    )
+    )(left_env[0], site[0], psi[0], right_env[0], table)
+    return new_left[None], product[None]
 
 
 def shifted(block, axis, distance):

time: 197 us -> 158 us (0.80)
  local copies, waits for them, and re-layouts: 23.5 us -> 5.3 us
  Pallas kernels: 168 us -> 150 us
  other arithmetic: 3.93 us -> 0 us
    pallas_call x1, Pallas kernels: 168 us -> 150 us  [fused(): pl.pallas_call(functools.partial(kernel, (rows, width, phys, chi, group,...]
    mul x2 -> x0, local copies, waits for them, and re-layouts: 8.77 us -> none  [fused(): mpo.transpose(3, 1, 2, 0)[:, :, None, :, None, :]]
    reshape x3 -> x1, local copies, waits for them, and re-layouts: 6.17 us -> 0.69 us  [fused(): table = mpo.transpose(3, 1, 2, 0).reshape(small, small)]
    mul x1 -> x0, other arithmetic: 3.92 us -> none  [fused(): mpo.transpose(3, 1, 2, 0)[:, :, None, :, None, :]]
    another operation x1 -> x0, local copies, waits for them, and re-layouts: 2.6 us -> none  [fused(): pairs = psi[0].reshape(rows, pq, cuts, step).transpose(2, 1, 0, 3)]
    unnamed x9 -> x4, local copies, waits for them, and re-layouts: 5.55 us -> 3.73 us
where the time goes in v2:
time: 158 us; the launch traced here: 156 us
  Pallas kernels  150 us (95%)
  local copies, waits for them, and re-layouts  5.3 us (3%)
    pallas_call x1, Pallas kernels, fused(): pl.pallas_call(functools.partial(kernel, (rows, width, phys, chi, group,...  150 us
    unnamed x4, local copies, waits for them, and re-layouts  3.73 us

profile of v2, /device:TPU:16, one launch (start us, length us, event | category | flops | bytes accessed | tf_op | source)
XLA Modules:
  0.0 155.6 jit_solution(3635285510279395310)
XLA Ops:
  0.6 0.9 copy.7
  1.5 0.7 reshape.7.mpo_h
  2.2 149.6 %shard_map.68 = (bf16[128,8,512]{2,1,0:T(8,128)(2,1)}, bf16[128,4,4,512]{3,2,1,0:T(4,128)(2,1)}) custom-call(bf16[128,8,512]{2,1,0:T(8,128)(2,1)} %bitcast.10, bf16[128,4,512]{2,1,0:T(4,128)(2,1)} %bitcast.12, bf16[128,4,4,512]{3,2,1,0:T(4,128)(2,1)} %bitcast.8, bf16[8,512,512]{2,1,0:T(8,128)(2,1)} %bitcast.7, bf16[32,32]{1,0:T(8,128)(2,1)} %reshape.7.mpo_h), custom_call_target="tpu_custom_call" | custom-call | tf_op jit(solution)/shard_map/pallas_call | solution.py:314
  151.9 0.0 copy-start
  151.9 2.4 %copy.10 = bf16[1,128,8,512]{3,2,1,0:T(8,128)(2,1)} copy(bf16[1,128,8,512]{3,2,1,0:T(8,128)(2,1)} %bitcast.11) | data formatting | bytes 2097152
  154.3 0.0 copy-done
  154.3 1.3 copy.11
Async XLA Ops:
  151.9 2.4 %copy-start = (bf16[128,4,4,512]{3,2,1,0:T(4,128)(2,1)S(1)}, bf16[128,4,4,512]{3,2,1,0:T(4,128)(2,1)}, u32[]{:S(2)}) copy-start(bf16[128,4,4,512]{3,2,1,0:T(4,128)(2,1)} %get-tuple-element.5) | copy-start | bytes 6291460

commit v3 on v2

--- a/solution.py
+++ b/solution.py
@@ -257,8 +257,7 @@
     for q in range(cuts):
         complete(q)
 
-        @pl.loop(0, rows // batch)
-        def _(g):
+        def strip_of(g):
             high = batch * width
             ours = nl_in[pl.ds(pl.multiple_of(g * high, high), high), :]
 
@@ -293,8 +292,12 @@
                 out = total.reshape(batch, phys, phys, chi).astype(BF16)
                 product[pl.ds(pl.multiple_of(g * batch, batch), batch)] = out
 
-        if q == 1:
-            relay(3)
+        if q == cuts - 2:
+            strip_of(0)
+            relay(cuts - 1)
+            pl.loop(1, rows // batch)(strip_of)
+        else:
+            pl.loop(0, rows // batch)(strip_of)
 
     for copy in started:
         copy.wait_send()

time: 158 us -> 158 us (level); the launches traced: 156 us -> 158 us
  Pallas kernels: 150 us -> 152 us
    pallas_call x1, Pallas kernels: 150 us -> 152 us  [fused(): pl.pallas_call(functools.partial(kernel, (rows, width, phys, chi, group,...]
where the time goes in v3:
time: 158 us
  Pallas kernels  152 us (96%)
  local copies, waits for them, and re-layouts  5.3 us (3%)
    pallas_call x1, Pallas kernels, fused(): pl.pallas_call(functools.partial(kernel, (rows, width, phys, chi, group,...  152 us
    unnamed x4, local copies, waits for them, and re-layouts  3.73 us

profile of v3, /device:TPU:16, one launch (start us, length us, event | category | flops | bytes accessed | tf_op | source)
XLA Modules:
  0.0 157.9 jit_solution(12787212160350096999)
XLA Ops:
  0.6 0.9 copy.7
  1.5 0.7 reshape.7.mpo_h
  2.2 151.9 %shard_map.68 = (bf16[128,8,512]{2,1,0:T(8,128)(2,1)}, bf16[128,4,4,512]{3,2,1,0:T(4,128)(2,1)}) custom-call(bf16[128,8,512]{2,1,0:T(8,128)(2,1)} %bitcast.10, bf16[128,4,512]{2,1,0:T(4,128)(2,1)} %bitcast.12, bf16[128,4,4,512]{3,2,1,0:T(4,128)(2,1)} %bitcast.8, bf16[8,512,512]{2,1,0:T(8,128)(2,1)} %bitcast.7, bf16[32,32]{1,0:T(8,128)(2,1)} %reshape.7.mpo_h), custom_call_target="tpu_custom_call" | custom-call | tf_op jit(solution)/shard_map/pallas_call | solution.py:317
  154.1 0.0 copy-start
  154.1 2.4 %copy.10 = bf16[1,128,8,512]{3,2,1,0:T(8,128)(2,1)} copy(bf16[1,128,8,512]{3,2,1,0:T(8,128)(2,1)} %bitcast.11) | data formatting | bytes 2097152
  156.5 0.0 copy-done
  156.5 1.3 copy.11
Async XLA Ops:
  154.1 2.4 %copy-start = (bf16[128,4,4,512]{3,2,1,0:T(4,128)(2,1)S(1)}, bf16[128,4,4,512]{3,2,1,0:T(4,128)(2,1)}, u32[]{:S(2)}) copy-start(bf16[128,4,4,512]{3,2,1,0:T(4,128)(2,1)} %get-tuple-element.5) | copy-start | bytes 6291460

commit v4 on v3

--- a/solution.py
+++ b/solution.py
@@ -200,7 +200,6 @@
                 where = pl.multiple_of(u * rows + g * group, group)
                 second[n, pl.ds(where, group), :] = out[at:at + group, :]
 
-    relay(0)
     half_w = width // 2
     order = [k + d * half_w for k in range(half_w) for d in range(2)]
 
@@ -219,7 +218,6 @@
             first_round(behind)
         behind = n
     first_round(behind)
-    spread(1)
 
     def second_round(n):
         if n < half_w:
@@ -236,8 +234,8 @@
             second_round(behind)
         behind = n
     second_round(behind)
-    relay(1)
-    spread(2)
+    relay(0)
+    spread(1)
     for n in order:
         src, last = (to_x, to_y) if n < half_w else (to_y, to_x)
         arrive(("rs_own", n), rs1.at[n, 0], src)
@@ -249,8 +247,8 @@
     nl_own[...] = whole.astype(BF16)
     new_left[...] = whole.reshape(rows, width, chi).astype(BF16)
     send("left", nl_own, nl_in, to_next)
-    relay(2)
-    spread(3)
+    relay(1)
+    spread(2)
     loads["right"].wait()
     arrive("left", nl_in, to_next)
 
@@ -292,9 +290,11 @@
                 out = total.reshape(batch, phys, phys, chi).astype(BF16)
                 product[pl.ds(pl.multiple_of(g * batch, batch), batch)] = out
 
-        if q == cuts - 2:
+        if 0 < q < cuts - 1:
             strip_of(0)
-            relay(cuts - 1)
+            relay(q + 1)
+            if q + 2 < cuts:
+                spread(q + 2)
             pl.loop(1, rows // batch)(strip_of)
         else:
             pl.loop(0, rows // batch)(strip_of)

time: 158 us -> 148 us (0.937)
  Pallas kernels: 152 us -> 141 us
    pallas_call x1, Pallas kernels: 152 us -> 141 us  [fused(): pl.pallas_call(functools.partial(kernel, (rows, width, phys, chi, group,...]
where the time goes in v4:
time: 148 us; the launch traced here: 147 us
  Pallas kernels  141 us (95%)
  local copies, waits for them, and re-layouts  5.3 us (4%)
    pallas_call x1, Pallas kernels, fused(): pl.pallas_call(functools.partial(kernel, (rows, width, phys, chi, group,...  141 us
    unnamed x4, local copies, waits for them, and re-layouts  3.73 us

profile of v4, /device:TPU:16, one launch (start us, length us, event | category | flops | bytes accessed | tf_op | source)
XLA Modules:
  0.0 147.4 jit_solution(18384994671334635302)
XLA Ops:
  0.6 0.9 copy.7
  1.5 0.7 reshape.7.mpo_h
  2.2 141.5 %shard_map.68 = (bf16[128,8,512]{2,1,0:T(8,128)(2,1)}, bf16[128,4,4,512]{3,2,1,0:T(4,128)(2,1)}) custom-call(bf16[128,8,512]{2,1,0:T(8,128)(2,1)} %bitcast.10, bf16[128,4,512]{2,1,0:T(4,128)(2,1)} %bitcast.12, bf16[128,4,4,512]{3,2,1,0:T(4,128)(2,1)} %bitcast.8, bf16[8,512,512]{2,1,0:T(8,128)(2,1)} %bitcast.7, bf16[32,32]{1,0:T(8,128)(2,1)} %reshape.7.mpo_h), custom_call_target="tpu_custom_call" | custom-call | tf_op jit(solution)/shard_map/pallas_call | solution.py:317
  143.7 0.0 copy-start
  143.7 2.4 %copy.10 = bf16[1,128,8,512]{3,2,1,0:T(8,128)(2,1)} copy(bf16[1,128,8,512]{3,2,1,0:T(8,128)(2,1)} %bitcast.11) | data formatting | bytes 2097152
  146.1 0.0 copy-done
  146.1 1.3 copy.11
Async XLA Ops:
  143.7 2.4 %copy-start = (bf16[128,4,4,512]{3,2,1,0:T(4,128)(2,1)S(1)}, bf16[128,4,4,512]{3,2,1,0:T(4,128)(2,1)}, u32[]{:S(2)}) copy-start(bf16[128,4,4,512]{3,2,1,0:T(4,128)(2,1)} %get-tuple-element.5) | copy-start | bytes 6291460

commit v5 on v4

--- a/solution.py
+++ b/solution.py
@@ -36,6 +36,7 @@
     bx = (me // 2) * 2 + 1 - lax.rem(me, 2)
     by = lax.rem(me + 2, n_bond)
     bd = lax.rem(bx + 2, n_bond)
+    x, y = lax.rem(me, 2), me // 2
     to_x = {"bond": bx}
     to_y = {"bond": by}
     to_next = {"sec": next_sec}
@@ -48,7 +49,7 @@
         ("site", site_h, site_raw),
         ("psi", psi_h, psi_raw),
         ("mpo", mpo_h, mpo),
-        ("left", left_h, left),
+        ("left", left_h, left.at[x]),
         ("right", right_h, right),
     )):
         loads[name] = pltpu.make_async_copy(src, dst, local_sem.at[i])
@@ -91,11 +92,11 @@
         for i in range(cuts):
             tile = acc[i, pl.ds(t, rows, stride=phys), :]
             site_own[t, :, i * lanes:(i + 1) * lanes] = tile.astype(BF16)
-            site_tr[i * lanes:(i + 1) * lanes, t * rows:(t + 1) * rows] = tile.T.astype(BF16)
+            site_tr[x, i * lanes:(i + 1) * lanes, t * rows:(t + 1) * rows] = tile.T.astype(BF16)
     site_here = pltpu.make_async_copy(site_own, site.at[:, block(me), :], local_sem.at[5])
     site_here.start()
     send("site_x", site_own, site.at[:, block(me), :], to_x)
-    send("site_y", site_own, site.at[:, block(me), :], to_y)
+    send("left_x", left_h, left.at[x], to_x)
 
     loads["psi"].wait()
     tall = 8
@@ -174,75 +175,77 @@
         both += near * mm(t2, one_hot(col_v * width + n == code_c))
     pair[...] = both.astype(BF16)
 
-    cut_s = phys // 2
-    lo, hi = pl.ds(0, cut_s), pl.ds(cut_s, phys - cut_s)
+    wide_b = chi // 2
+    cols = pl.ds(pl.multiple_of(x * wide_b, wide_b), wide_b)
+
+    def pair_rows(which):
+        return pl.ds(pl.multiple_of(which * 2 * rows, 2 * rows), 2 * rows)
+
+    site_here.wait()
     arrive("site_x", site.at[:, block(bx), :], to_x)
-    send("site_xy", site.at[lo, block(bx), :], site.at[lo, block(bx), :], to_y)
-    arrive("site_y", site.at[:, block(by), :], to_y)
-    send("site_yx", site.at[hi, block(by), :], site.at[hi, block(by), :], to_x)
+    ours = site.at[:, pair_rows(y), cols]
+    send("site_pair", ours, ours, to_y)
+    for t in range(phys):
+        for i in range(cuts):
+            tile = site[t, block(bx), i * lanes:(i + 1) * lanes].astype(F32)
+            place = (slice(i * lanes, (i + 1) * lanes), slice(t * rows, (t + 1) * rows))
+            site_tr[(1 - x,) + place] = tile.T.astype(BF16)
     spread(0)
     loads["left"].wait()
-    site_here.wait()
-    arrive("site_xy", site.at[lo, block(bd), :], to_y)
-    arrive("site_yx", site.at[hi, block(bd), :], to_x)
+    arrive("site_pair", site.at[:, pair_rows(1 - y), cols], to_y)
 
     strip = group * width
 
-    @pl.loop(0, rows // group)
-    def _(g):
-        ours = left[pl.ds(pl.multiple_of(g * group, group), group)].astype(F32)
-        ours = ours.reshape(strip, chi).astype(BF16)
-        first = jnp.concatenate([mm(ours, site[s]).astype(BF16) for s in range(phys)], axis=0)
-        out = mm(mix[...], first).astype(BF16)
-        for u in range(phys):
-            for n in range(width):
-                at = (u * width + n) * group
-                where = pl.multiple_of(u * rows + g * group, group)
-                second[n, pl.ds(where, group), :] = out[at:at + group, :]
-
-    half_w = width // 2
-    order = [k + d * half_w for k in range(half_w) for d in range(2)]
+    def fill(which):
+        @pl.loop(0, rows // group)
+        def _(g):
+            ours = left[which, pl.ds(pl.multiple_of(g * group, group), group)].astype(F32)
+            ours = ours.reshape(strip, chi).astype(BF16)
+            first = [mm(ours, site[t, :, cols]).astype(BF16) for t in range(phys)]
+            out = mm(mix[...], jnp.concatenate(first, axis=0)).astype(BF16)
+            for u in range(phys):
+                for n in range(width):
+                    at = (u * width + n) * group
+                    where = pl.multiple_of(u * rows + g * group, group)
+                    second[n, which, pl.ds(where, group), :] = out[at:at + group, :]
+
+    fill(x)
+    arrive("left_x", left.at[1 - x], to_x)
+    fill(1 - x)
 
     def first_round(n):
-        if n < half_w:
-            send(("rs_own", n), part.at[n, block(bx), :], rs1.at[n, 0], to_x)
-            send(("rs_far", n), part.at[n, block(bd), :], rs1.at[n, 1], to_x)
-        else:
-            send(("rs_own", n), part.at[n, block(by), :], rs1.at[n, 0], to_y)
-            send(("rs_far", n), part.at[n, block(bd), :], rs1.at[n, 1], to_y)
-
-    behind = None
-    for n in order:
-        part[n] = mm(site_tr[...], second[n]).astype(BF16)
-        if behind is not None:
-            first_round(behind)
-        behind = n
-    first_round(behind)
+        send(("rs", n), part.at[n, pair_rows(1 - y), :], rs1.at[n], to_y)
 
     def second_round(n):
-        if n < half_w:
-            send(("rs_last", n), send2.at[n], rs2.at[n], to_y)
-        else:
-            send(("rs_last", n), send2.at[n], rs2.at[n], to_x)
-
-    behind = None
-    for n in order:
-        src, other = (to_x, by) if n < half_w else (to_y, bx)
-        arrive(("rs_far", n), rs1.at[n, 1], src)
-        send2[n] = (part[n, block(other), :].astype(F32) + rs1[n, 1].astype(F32)).astype(BF16)
-        if behind is not None:
-            second_round(behind)
-        behind = n
-    second_round(behind)
+        send(("swap", n), send2.at[n], rs2.at[n], to_x)
+
+    for n in range(width):
+        part[n] = (mm(site_tr[0], second[n, 0]) + mm(site_tr[1], second[n, 1])).astype(BF16)
+        if n > 0:
+            first_round(n - 1)
+    first_round(width - 1)
+
+    def block_in_pair(which):
+        return pl.ds(pl.multiple_of(which * rows, rows), rows)
+
+    for n in range(width):
+        arrive(("rs", n), rs1.at[n], to_y)
+        far = part[n, block(bx), :].astype(F32) + rs1[n, block_in_pair(1 - x), :].astype(F32)
+        send2[n] = far.astype(BF16)
+        own = part[n, block(me), :].astype(F32) + rs1[n, block_in_pair(x), :].astype(F32)
+        for i in range(cuts // 2):
+            acc[x * (cuts // 2) + i, pl.ds(n, rows, stride=width), :] = own[:, i * lanes:(i + 1) * lanes]
+        if n > 0:
+            second_round(n - 1)
+    second_round(width - 1)
     relay(0)
     spread(1)
-    for n in order:
-        src, last = (to_x, to_y) if n < half_w else (to_y, to_x)
-        arrive(("rs_own", n), rs1.at[n, 0], src)
-        arrive(("rs_last", n), rs2.at[n], last)
-        total = part[n, block(me), :].astype(F32) + rs1[n, 0].astype(F32) + rs2[n].astype(F32)
-        for i in range(cuts):
-            acc[i, pl.ds(n, rows, stride=width), :] = total[:, i * lanes:(i + 1) * lanes]
+    for n in range(width):
+        arrive(("swap", n), rs2.at[n], to_x)
+        other = rs2[n].astype(F32)
+        for i in range(cuts // 2):
+            at = (1 - x) * (cuts // 2) + i
+            acc[at, pl.ds(n, rows, stride=width), :] = other[:, i * lanes:(i + 1) * lanes]
     whole = jnp.concatenate([acc[i, :rows * width, :] for i in range(cuts)], axis=1)
     nl_own[...] = whole.astype(BF16)
     new_left[...] = whole.reshape(rows, width, chi).astype(BF16)
@@ -323,7 +326,7 @@
         in_specs=[any_spec] * 5,
         out_specs=(vmem, vmem),
         scratch_shapes=[
-            pltpu.VMEM((rows, width, chi), BF16),
+            pltpu.VMEM((2, rows, width, chi), BF16),
             pltpu.VMEM((rows, phys, chi), BF16),
             pltpu.VMEM((rows, phys, phys, chi), BF16),
             pltpu.VMEM((small, small), BF16),
@@ -331,14 +334,14 @@
             pltpu.VMEM((phys, rows, chi), BF16),
             pltpu.VMEM((cuts, pq // 2, rows, 2 * lanes), BF16),
             pltpu.VMEM((phys, chi, chi), BF16),
-            pltpu.VMEM((chi, phys * rows), BF16),
+            pltpu.VMEM((2, chi, phys * rows), BF16),
             pltpu.VMEM((small * group, small * group), BF16),
             pltpu.VMEM((width * pq, width * pq), BF16),
-            pltpu.VMEM((width, phys * rows, chi), BF16),
-            pltpu.VMEM((width, chi, chi), BF16),
-            pltpu.VMEM((width, 2, rows, chi), BF16),
-            pltpu.VMEM((width, rows, chi), BF16),
-            pltpu.VMEM((width, rows, chi), BF16),
+            pltpu.VMEM((width, 2, phys * rows, chi // 2), BF16),
+            pltpu.VMEM((width, chi, chi // 2), BF16),
+            pltpu.VMEM((width, 2 * rows, chi // 2), BF16),
+            pltpu.VMEM((width, rows, chi // 2), BF16),
+            pltpu.VMEM((width, rows, chi // 2), BF16),
             pltpu.VMEM((rows * width, chi), BF16),
             pltpu.VMEM((rows * width, chi), BF16),
             pltpu.VMEM((cuts, pq // 2, chi, 2 * lanes), BF16),

time: 148 us -> 151 us (1.020)
  Pallas kernels: 141 us -> 145 us
    pallas_call x1, Pallas kernels: 141 us -> 145 us  [fused(): pl.pallas_call(functools.partial(kernel, (rows, width, phys, chi, group,...]
where the time goes in v5:
time: 151 us
  Pallas kernels  145 us (96%)
  local copies, waits for them, and re-layouts  5.3 us (4%)
    pallas_call x1, Pallas kernels, fused(): pl.pallas_call(functools.partial(kernel, (rows, width, phys, chi, group,...  145 us
    unnamed x4, local copies, waits for them, and re-layouts  3.73 us

profile of v5, /device:TPU:16, one launch (start us, length us, event | category | flops | bytes accessed | tf_op | source)
XLA Modules:
  0.0 150.9 jit_solution(8408817552599108303)
XLA Ops:
  0.6 0.9 copy.7
  1.5 0.7 reshape.7.mpo_h
  2.2 145.0 %shard_map.68 = (bf16[128,8,512]{2,1,0:T(8,128)(2,1)}, bf16[128,4,4,512]{3,2,1,0:T(4,128)(2,1)}) custom-call(bf16[128,8,512]{2,1,0:T(8,128)(2,1)} %bitcast.10, bf16[128,4,512]{2,1,0:T(4,128)(2,1)} %bitcast.12, bf16[128,4,4,512]{3,2,1,0:T(4,128)(2,1)} %bitcast.8, bf16[8,512,512]{2,1,0:T(8,128)(2,1)} %bitcast.7, bf16[32,32]{1,0:T(8,128)(2,1)} %reshape.7.mpo_h), custom_call_target="tpu_custom_call" | custom-call | tf_op jit(solution)/shard_map/pallas_call | solution.py:320
  147.2 0.0 copy-start
  147.2 2.4 %copy.10 = bf16[1,128,8,512]{3,2,1,0:T(8,128)(2,1)} copy(bf16[1,128,8,512]{3,2,1,0:T(8,128)(2,1)} %bitcast.11) | data formatting | bytes 2097152
  149.6 0.0 copy-done
  149.6 1.3 copy.11
Async XLA Ops:
  147.2 2.4 %copy-start = (bf16[128,4,4,512]{3,2,1,0:T(4,128)(2,1)S(1)}, bf16[128,4,4,512]{3,2,1,0:T(4,128)(2,1)}, u32[]{:S(2)}) copy-start(bf16[128,4,4,512]{3,2,1,0:T(4,128)(2,1)} %get-tuple-element.5) | copy-start | bytes 6291460

commit v6 on v5

--- a/solution.py
+++ b/solution.py
@@ -109,12 +109,12 @@
         for i in range(cuts):
             acc[i, where, :] = flat[:, i * lanes:(i + 1) * lanes]
 
-    half = pq // 4
+    halves = (pl.ds(0, 5 * pq // 16), pl.ds(5 * pq // 16, pq // 2 - 5 * pq // 16))
 
     def region(q, owner, sub=None):
         if sub is None:
             return psi.at[q, :, block(owner), :]
-        return psi.at[q, pl.ds(sub * half, half), block(owner), :]
+        return psi.at[q, halves[sub], block(owner), :]
 
     for q in range(cuts):
         for t in range(pq):
@@ -126,13 +126,25 @@
     send(("shift", cuts - 1), psi_own.at[cuts - 1], region(cuts - 1, me), to_next)
 
     def spread(q):
+        spread_x(q)
+        spread_y(q)
+
+    def spread_x(q):
         arrive(("shift", q), region(q, me), to_next)
         send(("psi_x", q), region(q, me), region(q, me), to_x)
+
+    def spread_y(q):
         send(("psi_y", q), region(q, me), region(q, me), to_y)
 
     def relay(q):
+        relay_y(q)
+        relay_x(q)
+
+    def relay_y(q):
         arrive(("psi_x", q), region(q, bx), to_x)
         send(("psi_xy", q), region(q, bx, 0), region(q, bx, 0), to_y)
+
+    def relay_x(q):
         arrive(("psi_y", q), region(q, by), to_y)
         send(("psi_yx", q), region(q, by, 1), region(q, by, 1), to_x)
 
@@ -224,6 +236,8 @@
         if n > 0:
             first_round(n - 1)
     first_round(width - 1)
+    relay_x(0)
+    spread_x(1)
 
     def block_in_pair(which):
         return pl.ds(pl.multiple_of(which * rows, rows), rows)
@@ -238,8 +252,8 @@
         if n > 0:
             second_round(n - 1)
     second_round(width - 1)
-    relay(0)
-    spread(1)
+    relay_y(0)
+    spread_y(1)
     for n in range(width):
         arrive(("swap", n), rs2.at[n], to_x)
         other = rs2[n].astype(F32)

time: 151 us -> 153 us (1.013)
  Pallas kernels: 145 us -> 147 us
    pallas_call x1, Pallas kernels: 145 us -> 147 us  [fused(): pl.pallas_call(functools.partial(kernel, (rows, width, phys, chi, group,...]
where the time goes in v6:
time: 153 us
  Pallas kernels  147 us (96%)
  local copies, waits for them, and re-layouts  5.3 us (3%)
    pallas_call x1, Pallas kernels, fused(): pl.pallas_call(functools.partial(kernel, (rows, width, phys, chi, group,...  147 us
    unnamed x4, local copies, waits for them, and re-layouts  3.73 us

profile of v6, /device:TPU:16, one launch (start us, length us, event | category | flops | bytes accessed | tf_op | source)
XLA Modules:
  0.0 152.7 jit_solution(4717397016386981906)
XLA Ops:
  0.6 0.9 copy.7
  1.5 0.7 reshape.7.mpo_h
  2.2 146.8 %shard_map.68 = (bf16[128,8,512]{2,1,0:T(8,128)(2,1)}, bf16[128,4,4,512]{3,2,1,0:T(4,128)(2,1)}) custom-call(bf16[128,8,512]{2,1,0:T(8,128)(2,1)} %bitcast.10, bf16[128,4,512]{2,1,0:T(4,128)(2,1)} %bitcast.12, bf16[128,4,4,512]{3,2,1,0:T(4,128)(2,1)} %bitcast.8, bf16[8,512,512]{2,1,0:T(8,128)(2,1)} %bitcast.7, bf16[32,32]{1,0:T(8,128)(2,1)} %reshape.7.mpo_h), custom_call_target="tpu_custom_call" | custom-call | tf_op jit(solution)/shard_map/pallas_call | solution.py:334
  149.0 0.0 copy-start
  149.0 2.4 %copy.10 = bf16[1,128,8,512]{3,2,1,0:T(8,128)(2,1)} copy(bf16[1,128,8,512]{3,2,1,0:T(8,128)(2,1)} %bitcast.11) | data formatting | bytes 2097152
  151.4 0.0 copy-done
  151.4 1.3 copy.11
Async XLA Ops:
  149.0 2.4 %copy-start = (bf16[128,4,4,512]{3,2,1,0:T(4,128)(2,1)S(1)}, bf16[128,4,4,512]{3,2,1,0:T(4,128)(2,1)}, u32[]{:S(2)}) copy-start(bf16[128,4,4,512]{3,2,1,0:T(4,128)(2,1)} %get-tuple-element.5) | copy-start | bytes 6291460
